TPU v7x, 32 devices: a whole 2x2x4 slice. The times are simulated.
32 devices in a mesh: row: 8 (over z, x), col: 4 (over y, core).
Axes of the slice: x: 2, y: 2, z: 4, core: 2. Of those that a mesh axis runs over, the one named last changes fastest.
Arguments:
- features: bfloat16 [8192, 256], P(('row', 'col')), may hold values from -6 to 6
- grad_out: bfloat16 [8192, 256], P(('row', 'col')), may hold values from -6 to 6
- degrees: int32 [8192], P(('row', 'col')), may hold values from 1 to 8236, as said below
- w_self: bfloat16 [256, 256], replicated, may hold values from -0.375 to 0.375
- w_neigh: bfloat16 [256, 256], replicated, may hold values from -0.375 to 0.375
- bias: float32 [256], replicated, may hold values from -4 to 4
- tile_slots: int32 [8, 4, 88], P('row', 'col'), may hold values from 0 to 127, as said below
- tile_count: int32 [8, 4], P('row', 'col'), may hold values from 22 to 88, as said below
- tile_masks: int32 [8, 4, 88, 16, 128], P('row', 'col'), may hold values from 0 to 255
Outputs:
- layer_out: bfloat16 [8192, 256], P(('row', 'col'))
- grad_in: bfloat16 [8192, 256], P(('row', 'col'))
- grad_w_self: float32 [256, 256], replicated
- grad_w_neigh: float32 [256, 256], replicated
Inputs may be any that keep to these rules, and one draw needn't show every extreme that they name: `tile_slots`: on each device the 88 slot numbers are distinct and rise; slot s names block row s % 8 of the device's row group and block column s // 8 of its panel. Only a device's first tile_count tiles are live; the others are ignored. Some device holds 88 live tiles. `degrees`: each node's degree is at least the number of ones in its row of A, and at least 1; some node has the largest degree.
All inputs are finite; a program needn't handle non-finite values.
Results may differ from a plain program's by a relative error of at most 0.014.
Values may be sent and summed in bfloat16 or wider, within the bound.
No kernel may reach another device: no remote copies, remote signals or barrier semaphores. Data moves between devices by JAX's collectives and lax.ppermute only.
A program may use at most 64 MiB of HBM per device.

v0:
```python
import math
import jax
import jax.numpy as jnp
from jax import lax
from jax.sharding import PartitionSpec as P

group_tiles = 8


def unpack_tiles(mask_words):
    shifts = jnp.arange(8, dtype=jnp.int32)
    bit_values = jnp.bitwise_and(
        jnp.right_shift(mask_words[:, :, None, :], shifts[None, None, :, None]), 1
    )
    return bit_values.reshape(mask_words.shape[0], mask_words.shape[1] * 8, mask_words.shape[2])


def tile_range(slot_ids, live_count, block_rows, low_column, high_column, tile_width):
    column_block = slot_ids // block_rows
    positions = jnp.arange(slot_ids.shape[0], dtype=jnp.int32)
    is_live = positions < live_count
    first_tile = jnp.sum(
        jnp.logical_and(is_live, (column_block + 1) * tile_width <= low_column).astype(jnp.int32)
    )
    last_tile = jnp.sum(
        jnp.logical_and(is_live, column_block * tile_width < high_column).astype(jnp.int32)
    )
    return (first_tile, last_tile)


def aggregate_piece(totals, panel_piece, first_row, slot_ids, live_count, mask_words):
    tile_width = mask_words.shape[2]
    block_rows = totals.shape[0] // tile_width
    piece_rows = panel_piece.shape[0]
    feature_width = panel_piece.shape[1]
    first_tile, last_tile = tile_range(
        slot_ids, live_count, block_rows, first_row, first_row + piece_rows, tile_width
    )
    margin = jnp.zeros((tile_width, feature_width), panel_piece.dtype)
    padded = jnp.concatenate([margin, panel_piece, margin], axis=0)
    group_count = (last_tile - first_tile + group_tiles - 1) // group_tiles
    within = jnp.arange(group_tiles, dtype=jnp.int32)
    tile_columns = jnp.arange(tile_width, dtype=jnp.int32)

    def aggregate_one_group(group_index, running):
        chosen = first_tile + group_index * group_tiles + within
        in_range = chosen < last_tile
        chosen = jnp.minimum(chosen, slot_ids.shape[0] - 1)
        chosen_slots = slot_ids[chosen]
        row_block = chosen_slots % block_rows
        column_block = chosen_slots // block_rows
        columns = column_block[:, None] * tile_width + tile_columns[None, :]
        keep_mask = in_range[:, None] & (columns >= first_row) & (columns < first_row + piece_rows)
        tile_bits = unpack_tiles(mask_words[chosen]) * keep_mask[:, :, None].astype(jnp.int32)
        offsets = column_block * tile_width - first_row + tile_width
        blocks = jax.vmap(lambda offset: lax.dynamic_slice_in_dim(padded, offset, tile_width, 0))(
            offsets
        )
        products = jnp.einsum(
            "gji,gjf->gif",
            tile_bits.astype(jnp.bfloat16),
            blocks,
            preferred_element_type=jnp.float32,
        )
        shaped = running.reshape(block_rows, tile_width, feature_width)
        return shaped.at[row_block].add(products).reshape(running.shape)

    return lax.fori_loop(0, group_count, aggregate_one_group, totals)


def spread_rows(first_row, row_count, slot_ids, live_count, mask_words, upward_rows):
    tile_width = mask_words.shape[2]
    block_rows = upward_rows.shape[0] // tile_width
    feature_width = upward_rows.shape[1]
    first_tile, last_tile = tile_range(
        slot_ids, live_count, block_rows, first_row, first_row + row_count, tile_width
    )
    first_block = first_row // tile_width
    upward_blocks = upward_rows.reshape(block_rows, tile_width, feature_width)
    group_count = (last_tile - first_tile + group_tiles - 1) // group_tiles
    within = jnp.arange(group_tiles, dtype=jnp.int32)

    def spread_one_group(group_index, running):
        chosen = first_tile + group_index * group_tiles + within
        in_range = chosen < last_tile
        chosen = jnp.minimum(chosen, slot_ids.shape[0] - 1)
        chosen_slots = slot_ids[chosen]
        row_block = chosen_slots % block_rows
        column_block = chosen_slots // block_rows
        tile_bits = unpack_tiles(mask_words[chosen]) * in_range[:, None, None].astype(jnp.int32)
        sources = upward_blocks[row_block]
        products = jnp.einsum(
            "gji,gif->gjf",
            tile_bits.astype(jnp.bfloat16),
            sources,
            preferred_element_type=jnp.float32,
        )
        return running.at[column_block - first_block].add(products)

    initial = jnp.zeros((row_count // tile_width, tile_width, feature_width), jnp.float32)
    partial_value = lax.fori_loop(0, group_count, spread_one_group, initial)
    return partial_value.reshape(row_count, feature_width)


def shards(features, grad_out, degrees, w_self, w_neigh, bias, tile_slots, tile_count, tile_masks):
    slot_ids = tile_slots[0, 0]
    live_count = tile_count[0, 0]
    mask_words = tile_masks[0, 0]
    node_rows, feature_width = features.shape
    group_size = node_rows * lax.axis_size("col")
    initial = jnp.zeros((group_size, feature_width), jnp.float32)
    panel = lax.all_gather(features, "row", axis=0, tiled=True)
    partial_value = aggregate_piece(initial, panel, 0, slot_ids, live_count, mask_words)
    summed = lax.psum_scatter(
        partial_value.astype(jnp.bfloat16), "col", scatter_dimension=0, tiled=True
    ).astype(jnp.float32)
    scale_degree = degrees.astype(jnp.float32)[:, None]
    mean_rows = (summed / scale_degree).astype(jnp.bfloat16)
    preact = jnp.dot(features, w_self, preferred_element_type=jnp.float32)
    preact = preact + jnp.dot(mean_rows, w_neigh, preferred_element_type=jnp.float32) + bias
    sigmoid_values = jax.nn.sigmoid(preact)
    layer_out = (preact * sigmoid_values).astype(jnp.bfloat16)
    grad_preact = (
        grad_out.astype(jnp.float32) * sigmoid_values * (1.0 + preact * (1.0 - sigmoid_values))
    ).astype(jnp.bfloat16)
    contract_rows = (((0,), (0,)), ((), ()))
    contract_cols = (((1,), (1,)), ((), ()))
    grad_self = lax.dot_general(
        features, grad_preact, contract_rows, preferred_element_type=jnp.float32
    )
    grad_neigh = lax.dot_general(
        mean_rows, grad_preact, contract_rows, preferred_element_type=jnp.float32
    )
    grad_self, grad_neigh = lax.psum((grad_self, grad_neigh), ("row", "col"))
    grad_scale = 1.0 / math.sqrt(node_rows * lax.axis_size("row") * lax.axis_size("col"))
    upward = lax.dot_general(
        grad_preact, w_neigh, contract_cols, preferred_element_type=jnp.float32
    )
    upward = (upward / scale_degree).astype(jnp.bfloat16)
    upward_rows = lax.all_gather(upward, "col", axis=0, tiled=True)
    panel_size = node_rows * lax.axis_size("row")
    neighbor_grad = lax.psum_scatter(
        spread_rows(0, panel_size, slot_ids, live_count, mask_words, upward_rows).astype(
            jnp.bfloat16
        ),
        "row",
        scatter_dimension=0,
        tiled=True,
    ).astype(jnp.float32)
    self_grad = lax.dot_general(
        grad_preact, w_self, contract_cols, preferred_element_type=jnp.float32
    )
    grad_in = (self_grad + neighbor_grad).astype(jnp.bfloat16)
    return (layer_out, grad_in, grad_self * grad_scale, grad_neigh * grad_scale)


def solution(mesh):
    placed = (
        P(("row", "col"), None),
        P(("row", "col"), None),
        P(("row", "col")),
        P(),
        P(),
        P(),
        P("row", "col", None),
        P("row", "col"),
        P("row", "col", None, None, None),
    )
    return jax.shard_map(
        shards,
        mesh=mesh,
        in_specs=placed,
        out_specs=(P(("row", "col"), None), P(("row", "col"), None), P(), P()),
        check_vma=False,
    )
```

profile of v0, /device:TPU:0, one launch (start us, length us, event | category | flops | bytes accessed | tf_op | source)
XLA Modules:
  0.0 546.3 jit_solution(3008152126363309649)
XLA Ops:
  11.3 41.9 %all-gather.2.cloned.1.call-done = bf16[2048,256]{1,0:T(8,128)(2,1)} async-done(((bf16[256,256]{1,0:T(8,128)(2,1)}), bf16[2048,256]{1,0:T(8,128)(2,1)}) %all-gather.2.cloned.1.call-update) | async-done | bytes 1048592 | tf_op jit(solution)/shard_map/all_gather | solution.py:112
  55.6 253.4 %while.30 = (s32[]{:T(128)}, f32[1024,256]{1,0:T(8,128)S(1)}, s32[]{:T(128)}, s32[]{:T(128)}, s32[88]{0:T(128)S(1)}, /*index=5*/s32[88,16,128]{2,1,0:T(8,128)}, ...) while((s32[]{:T(128)}, f32[1024,256]{1,0:T(8,128)S(1)}, ...), condition=%wide.region_4.5_spmd.clone, body=%wide.region_2.4_spmd.clone.sunk | while | flops 67902872 | bytes 5061454 | solution.py:68
  57.0 17.3 %while.32 = (s32[]{:T(128)}, bf16[2304,256]{1,0:T(8,128)(2,1)}, s32[8,2]{0,1:T(2,128)S(1)}, bf16[8,128,256]{2,1,0:T(8,128)(2,1)S(1)}, s32[]{:T(128)}) while((s32[]{:T(128)}, bf16[2304,256]{1,0:T(8,128)(2,1)}, s32[8,2]{0,1:T(2,128)S(1)}, bf16[8,128,256]{2,1,0:T(8,128)(2,1)S(1)}, s32[]{:T(128)}) %tuple.84), condition=%wide.while_cond, body=%wide.while_body.sunk | while | flops 2 | bytes 131177 | solution.py:56
  80.0 17.3 %while.32 = (s32[]{:T(128)}, bf16[2304,256]{1,0:T(8,128)(2,1)}, s32[8,2]{0,1:T(2,128)S(1)}, bf16[8,128,256]{2,1,0:T(8,128)(2,1)S(1)}, s32[]{:T(128)}) while((s32[]{:T(128)}, bf16[2304,256]{1,0:T(8,128)(2,1)}, s32[8,2]{0,1:T(2,128)S(1)}, bf16[8,128,256]{2,1,0:T(8,128)(2,1)S(1)}, s32[]{:T(128)}) %tuple.84), condition=%wide.while_cond, body=%wide.while_body.sunk | while | flops 2 | bytes 131177 | solution.py:56
  103.1 17.3 %while.32 = (s32[]{:T(128)}, bf16[2304,256]{1,0:T(8,128)(2,1)}, s32[8,2]{0,1:T(2,128)S(1)}, bf16[8,128,256]{2,1,0:T(8,128)(2,1)S(1)}, s32[]{:T(128)}) while((s32[]{:T(128)}, bf16[2304,256]{1,0:T(8,128)(2,1)}, s32[8,2]{0,1:T(2,128)S(1)}, bf16[8,128,256]{2,1,0:T(8,128)(2,1)S(1)}, s32[]{:T(128)}) %tuple.84), condition=%wide.while_cond, body=%wide.while_body.sunk | while | flops 2 | bytes 131177 | solution.py:56
  126.1 17.3 %while.32 = (s32[]{:T(128)}, bf16[2304,256]{1,0:T(8,128)(2,1)}, s32[8,2]{0,1:T(2,128)S(1)}, bf16[8,128,256]{2,1,0:T(8,128)(2,1)S(1)}, s32[]{:T(128)}) while((s32[]{:T(128)}, bf16[2304,256]{1,0:T(8,128)(2,1)}, s32[8,2]{0,1:T(2,128)S(1)}, bf16[8,128,256]{2,1,0:T(8,128)(2,1)S(1)}, s32[]{:T(128)}) %tuple.84), condition=%wide.while_cond, body=%wide.while_body.sunk | while | flops 2 | bytes 131177 | solution.py:56
  149.2 17.3 %while.32 = (s32[]{:T(128)}, bf16[2304,256]{1,0:T(8,128)(2,1)}, s32[8,2]{0,1:T(2,128)S(1)}, bf16[8,128,256]{2,1,0:T(8,128)(2,1)S(1)}, s32[]{:T(128)}) while((s32[]{:T(128)}, bf16[2304,256]{1,0:T(8,128)(2,1)}, s32[8,2]{0,1:T(2,128)S(1)}, bf16[8,128,256]{2,1,0:T(8,128)(2,1)S(1)}, s32[]{:T(128)}) %tuple.84), condition=%wide.while_cond, body=%wide.while_body.sunk | while | flops 2 | bytes 131177 | solution.py:56
  172.2 17.3 %while.32 = (s32[]{:T(128)}, bf16[2304,256]{1,0:T(8,128)(2,1)}, s32[8,2]{0,1:T(2,128)S(1)}, bf16[8,128,256]{2,1,0:T(8,128)(2,1)S(1)}, s32[]{:T(128)}) while((s32[]{:T(128)}, bf16[2304,256]{1,0:T(8,128)(2,1)}, s32[8,2]{0,1:T(2,128)S(1)}, bf16[8,128,256]{2,1,0:T(8,128)(2,1)S(1)}, s32[]{:T(128)}) %tuple.84), condition=%wide.while_cond, body=%wide.while_body.sunk | while | flops 2 | bytes 131177 | solution.py:56
  195.2 17.3 %while.32 = (s32[]{:T(128)}, bf16[2304,256]{1,0:T(8,128)(2,1)}, s32[8,2]{0,1:T(2,128)S(1)}, bf16[8,128,256]{2,1,0:T(8,128)(2,1)S(1)}, s32[]{:T(128)}) while((s32[]{:T(128)}, bf16[2304,256]{1,0:T(8,128)(2,1)}, s32[8,2]{0,1:T(2,128)S(1)}, bf16[8,128,256]{2,1,0:T(8,128)(2,1)S(1)}, s32[]{:T(128)}) %tuple.84), condition=%wide.while_cond, body=%wide.while_body.sunk | while | flops 2 | bytes 131177 | solution.py:56
  218.3 17.3 %while.32 = (s32[]{:T(128)}, bf16[2304,256]{1,0:T(8,128)(2,1)}, s32[8,2]{0,1:T(2,128)S(1)}, bf16[8,128,256]{2,1,0:T(8,128)(2,1)S(1)}, s32[]{:T(128)}) while((s32[]{:T(128)}, bf16[2304,256]{1,0:T(8,128)(2,1)}, s32[8,2]{0,1:T(2,128)S(1)}, bf16[8,128,256]{2,1,0:T(8,128)(2,1)S(1)}, s32[]{:T(128)}) %tuple.84), condition=%wide.while_cond, body=%wide.while_body.sunk | while | flops 2 | bytes 131177 | solution.py:56
  241.3 17.3 %while.32 = (s32[]{:T(128)}, bf16[2304,256]{1,0:T(8,128)(2,1)}, s32[8,2]{0,1:T(2,128)S(1)}, bf16[8,128,256]{2,1,0:T(8,128)(2,1)S(1)}, s32[]{:T(128)}) while((s32[]{:T(128)}, bf16[2304,256]{1,0:T(8,128)(2,1)}, s32[8,2]{0,1:T(2,128)S(1)}, bf16[8,128,256]{2,1,0:T(8,128)(2,1)S(1)}, s32[]{:T(128)}) %tuple.84), condition=%wide.while_cond, body=%wide.while_body.sunk | while | flops 2 | bytes 131177 | solution.py:56
  264.3 17.3 %while.32 = (s32[]{:T(128)}, bf16[2304,256]{1,0:T(8,128)(2,1)}, s32[8,2]{0,1:T(2,128)S(1)}, bf16[8,128,256]{2,1,0:T(8,128)(2,1)S(1)}, s32[]{:T(128)}) while((s32[]{:T(128)}, bf16[2304,256]{1,0:T(8,128)(2,1)}, s32[8,2]{0,1:T(2,128)S(1)}, bf16[8,128,256]{2,1,0:T(8,128)(2,1)S(1)}, s32[]{:T(128)}) %tuple.84), condition=%wide.while_cond, body=%wide.while_body.sunk | while | flops 2 | bytes 131177 | solution.py:56
  287.4 17.3 %while.32 = (s32[]{:T(128)}, bf16[2304,256]{1,0:T(8,128)(2,1)}, s32[8,2]{0,1:T(2,128)S(1)}, bf16[8,128,256]{2,1,0:T(8,128)(2,1)S(1)}, s32[]{:T(128)}) while((s32[]{:T(128)}, bf16[2304,256]{1,0:T(8,128)(2,1)}, s32[8,2]{0,1:T(2,128)S(1)}, bf16[8,128,256]{2,1,0:T(8,128)(2,1)S(1)}, s32[]{:T(128)}) %tuple.84), condition=%wide.while_cond, body=%wide.while_body.sunk | while | flops 2 | bytes 131177 | solution.py:56
  310.2 20.3 %reduce-scatter.3.cloned.1.call-done = bf16[256,256]{1,0:T(8,128)(2,1)} async-done(((bf16[1024,256]{1,0:T(8,128)(2,1)}), bf16[256,256]{1,0:T(8,128)(2,1)}) %reduce-scatter.3.cloned.1.call-update) | async-done | bytes 131088 | tf_op jit(solution)/shard_map/reduce_scatter | solution.py:114
  333.6 6.6 %all_gather.7 = bf16[1024,256]{1,0:T(8,128)(2,1)S(1)} all-gather(bf16[256,256]{1,0:T(8,128)(2,1)S(1)} %fusion.42), channel_id=1, replica_groups=mesh['row'=8,'col'=4] {'col'}, dimensions={0}, use_global_device_ids=true | all-gather | bytes 655360 | tf_op jit(solution)/shard_map/all_gather | solution.py:140
  342.8 87.3 %while.31 = (s32[]{:T(128)}, f32[16,128,256]{2,1,0:T(8,128)}, s32[]{:T(128)}, s32[]{:T(128)}, s32[88]{0:T(128)S(1)}, /*index=5*/s32[88,16,128]{2,1,0:T(8,128)}, ...) while((s32[]{:T(128)}, f32[16,128,256]{2,1,0:T(8,128)}, s32[]{:T(128)}, ...), condition=%wide.region_8.9_spmd.clone, body=%wide.region_6.8_spmd.clone.sunk | while | flops 67897608 | bytes 5974609 | solution.py:101
  347.5 3.3 scatter_fusion
  386.7 3.3 scatter_fusion
  394.7 3.4 scatter_fusion
  402.8 3.4 scatter_fusion
  418.7 3.3 scatter_fusion
  426.6 3.5 scatter_fusion
  432.8 38.5 %all-reduce.4.cloned.1.call-done = (f32[256,256]{0,1:T(8,128)}, f32[256,256]{0,1:T(8,128)}) async-done(((f32[256,256]{0,1:T(8,128)}, f32[256,256]{0,1:T(8,128)}), (f32[256,256]{0,1:T(8,128)}, f32[256,256]{0,1:T(8,128)})) %all-reduce.4.cloned.1.call-update) | async-done | bytes 524304 | tf_op jit(solution)/shard_map/psum | solution.py:134
  474.1 63.9 %reduce-scatter.5.cloned.1.call-done = bf16[256,256]{1,0:T(8,128)(2,1)} async-done(((bf16[2048,256]{1,0:T(8,128)(2,1)}), bf16[256,256]{1,0:T(8,128)(2,1)}) %reduce-scatter.5.cloned.1.call-update) | async-done | bytes 131088 | tf_op jit(solution)/shard_map/reduce_scatter | solution.py:142
  (585 shorter events, 320.8 us)
Async XLA Ops:
  7.2 323.3 %copy-start = (bf16[256,256]{1,0:T(8,128)(2,1)S(1)}, bf16[256,256]{1,0:T(8,128)(2,1)}, u32[]{:S(2)}) copy-start(bf16[256,256]{1,0:T(8,128)(2,1)} %param.17) | copy-start | bytes 393220
  7.2 48.4 %copy-start.1 = (s32[1,1,88]{2,1,0:T(1,128)S(1)}, s32[1,1,88]{2,1,0:T(1,128)}, u32[]{:S(2)}) copy-start(s32[1,1,88]{2,1,0:T(1,128)} %param.19) | copy-start | bytes 1060
  7.2 46.0 %all-gather.2.cloned.1.call-start = ((), (), s32[]{:S(2)}) async-start(), calls=%async_computation.2 | async-start | bytes 1179648 | tf_op jit(solution)/shard_map/all_gather | solution.py:112
  7.9 322.6 %reduce-scatter.3.cloned.1.call-start = ((), (), s32[]{:S(2)}) async-start(), calls=%async_computation.3 | async-start | bytes 655360 | tf_op jit(solution)/shard_map/reduce_scatter | solution.py:114
  309.0 1.0 copy-start.4
  309.0 1.0 copy-start.2
  309.0 1.0 copy-start.3
  309.0 21.5 %copy-start.5 = (bf16[256,256]{1,0:T(8,128)(2,1)S(1)}, bf16[256,256]{1,0:T(8,128)(2,1)}, u32[]{:S(2)}) copy-start(bf16[256,256]{1,0:T(8,128)(2,1)} %param.14) | copy-start | bytes 393220
  309.0 21.4 %copy-start.7 = (f32[256]{0:T(256)S(1)}, f32[256]{0:T(256)}, u32[]{:S(2)}) copy-start(f32[256]{0:T(256)} %param.18) | copy-start | bytes 3076
  309.9 161.4 %all-reduce.4.cloned.1.call-start = ((), (), s32[]{:S(2)}) async-start(), calls=%async_computation.5 | async-start | bytes 1048576 | tf_op jit(solution)/shard_map/psum | solution.py:134
  330.5 9.7 %copy-start.6 = (bf16[256,256]{1,0:T(8,128)(2,1)S(1)}, bf16[256,256]{1,0:T(8,128)(2,1)}, u32[]{:S(2)}) copy-start(bf16[256,256]{1,0:T(8,128)(2,1)} %reduce-scatter.3.cloned.1.call-done) | copy-start | bytes 393220
  341.2 196.7 %reduce-scatter.5.cloned.1.call-start = ((), (), s32[]{:S(2)}) async-start(), calls=%async_computation.4 | async-start | bytes 1179648 | tf_op jit(solution)/shard_map/reduce_scatter | solution.py:142
Sparse Core Ops, SparseCore 0:
  10.1 42.9 all-gather.1
  310.1 20.3 reduce-scatter.2
  341.3 129.9 all-reduce.3
  474.6 63.3 reduce-scatter.4
where the time goes:
time: 553 us; the launch traced here: 546 us
  local copies, waits for them, and re-layouts  251 us (45%)
  waiting for transfers between devices  165 us (30%)
  other arithmetic  72.9 us (13%)
  loops' own time  18.5 us (3%)
  matrix products  16.1 us (3%)
  between operations  15.8 us (3%)
  blocking collectives  6.59 us (1%)
    gather x264, local copies, waits for them, and re-layouts  188 us
    reduce_scatter x1, waiting for transfers between devices, shards(): lax.psum_scatter(spread_rows(0, panel_size, slot_ids, live_count, mask_wo...  63.9 us
    all_gather x1, waiting for transfers between devices, shards(): panel = lax.all_gather(features, 'row', axis=0, tiled=True)  41.9 us
    psum x1, waiting for transfers between devices, shards(): grad_self, grad_neigh = lax.psum((grad_self, grad_neigh), ('row', 'col'))  38.5 us
    scatter-add x11, other arithmetic, spread_one_group(): return running.at[column_block - first_block].add(products)  35.9 us
    reduce_scatter x1, waiting for transfers between devices, shards(): lax.psum_scatter(partial_value.astype(jnp.bfloat16), 'col', scatter_dimen...  20.3 us
    gather x11, local copies, waits for them, and re-layouts, spread_one_group(): mask_words[chosen]  18.3 us
    gather x11, local copies, waits for them, and re-layouts, aggregate_one_group(): mask_words[chosen]  18.3 us
  transfers between devices with their start and end apart: 4, of which 4 were waited for; matrix products, arithmetic and copies ran while one was open for 16% of the time, Pallas kernels for 0%

commit v1 on v0

--- a/solution.py
+++ b/solution.py
@@ -131,7 +131,7 @@
     grad_neigh = lax.dot_general(
         mean_rows, grad_preact, contract_rows, preferred_element_type=jnp.float32
     )
-    grad_self, grad_neigh = lax.psum((grad_self, grad_neigh), ("row", "col"))
+    grad_self, grad_neigh = lax.psum(lax.psum((grad_self, grad_neigh), "col"), "row")
     grad_scale = 1.0 / math.sqrt(node_rows * lax.axis_size("row") * lax.axis_size("col"))
     upward = lax.dot_general(
         grad_preact, w_neigh, contract_cols, preferred_element_type=jnp.float32

time: 553 us -> 539 us (0.975)
  waiting for transfers between devices: 165 us -> 152 us
    psum x1 -> x2, waiting for transfers between devices: 38.5 us -> 26.8 us  [the longest x1 26.8 us: shards(): lax.psum((grad_self, grad_neigh), 'col')]
  transfers between devices with their start and end apart: 4 -> 5, of which waited for: 4 -> 4; matrix products, arithmetic and copies ran while one was open for 16% -> 16% of each run, Pallas kernels for 0% -> 0%
where the time goes in v1:
time: 539 us; the launch traced here: 532 us
  local copies, waits for them, and re-layouts  251 us (47%)
  waiting for transfers between devices  152 us (28%)
  other arithmetic  72.8 us (14%)
  loops' own time  18.2 us (3%)
  matrix products  16.1 us (3%)
  between operations  15.8 us (3%)
  blocking collectives  6.61 us (1%)
    gather x264, local copies, waits for them, and re-layouts  188 us
    reduce_scatter x1, waiting for transfers between devices, shards(): lax.psum_scatter(spread_rows(0, panel_size, slot_ids, live_count, mask_wo...  61.9 us
    all_gather x1, waiting for transfers between devices, shards(): panel = lax.all_gather(features, 'row', axis=0, tiled=True)  41.9 us
    scatter-add x11, other arithmetic, spread_one_group(): return running.at[column_block - first_block].add(products)  35.7 us
    psum x1, waiting for transfers between devices, shards(): lax.psum((grad_self, grad_neigh), 'col')  26.8 us
    reduce_scatter x1, waiting for transfers between devices, shards(): lax.psum_scatter(partial_value.astype(jnp.bfloat16), 'col', scatter_dimen...  20.2 us
    gather x11, local copies, waits for them, and re-layouts, spread_one_group(): mask_words[chosen]  18.3 us
    gather x11, local copies, waits for them, and re-layouts, aggregate_one_group(): mask_words[chosen]  18.3 us
  transfers between devices with their start and end apart: 5, of which 4 were waited for; matrix products, arithmetic and copies ran while one was open for 16% of the time, Pallas kernels for 0%

profile of v1, /device:TPU:0, one launch (start us, length us, event | category | flops | bytes accessed | tf_op | source)
XLA Modules:
  0.0 532.3 jit_solution(8729226653921984026)
XLA Ops:
  11.3 41.9 %all-gather.2.cloned.1.call-done = bf16[2048,256]{1,0:T(8,128)(2,1)} async-done(((bf16[256,256]{1,0:T(8,128)(2,1)}), bf16[2048,256]{1,0:T(8,128)(2,1)}) %all-gather.2.cloned.1.call-update) | async-done | bytes 1048592 | tf_op jit(solution)/shard_map/all_gather | solution.py:112
  55.6 253.3 %while.30 = (s32[]{:T(128)}, f32[1024,256]{1,0:T(8,128)S(1)}, s32[]{:T(128)}, s32[]{:T(128)}, s32[88]{0:T(128)S(1)}, /*index=5*/s32[88,16,128]{2,1,0:T(8,128)}, ...) while((s32[]{:T(128)}, f32[1024,256]{1,0:T(8,128)S(1)}, ...), condition=%wide.region_4.5_spmd.clone, body=%wide.region_2.4_spmd.clone.sunk | while | flops 67902872 | bytes 5061454 | solution.py:68
  57.0 17.3 %while.32 = (s32[]{:T(128)}, bf16[2304,256]{1,0:T(8,128)(2,1)}, s32[8,2]{0,1:T(2,128)S(1)}, bf16[8,128,256]{2,1,0:T(8,128)(2,1)S(1)}, s32[]{:T(128)}) while((s32[]{:T(128)}, bf16[2304,256]{1,0:T(8,128)(2,1)}, s32[8,2]{0,1:T(2,128)S(1)}, bf16[8,128,256]{2,1,0:T(8,128)(2,1)S(1)}, s32[]{:T(128)}) %tuple.84), condition=%wide.while_cond, body=%wide.while_body.sunk | while | flops 2 | bytes 131177 | solution.py:56
  80.0 17.3 %while.32 = (s32[]{:T(128)}, bf16[2304,256]{1,0:T(8,128)(2,1)}, s32[8,2]{0,1:T(2,128)S(1)}, bf16[8,128,256]{2,1,0:T(8,128)(2,1)S(1)}, s32[]{:T(128)}) while((s32[]{:T(128)}, bf16[2304,256]{1,0:T(8,128)(2,1)}, s32[8,2]{0,1:T(2,128)S(1)}, bf16[8,128,256]{2,1,0:T(8,128)(2,1)S(1)}, s32[]{:T(128)}) %tuple.84), condition=%wide.while_cond, body=%wide.while_body.sunk | while | flops 2 | bytes 131177 | solution.py:56
  103.0 17.3 %while.32 = (s32[]{:T(128)}, bf16[2304,256]{1,0:T(8,128)(2,1)}, s32[8,2]{0,1:T(2,128)S(1)}, bf16[8,128,256]{2,1,0:T(8,128)(2,1)S(1)}, s32[]{:T(128)}) while((s32[]{:T(128)}, bf16[2304,256]{1,0:T(8,128)(2,1)}, s32[8,2]{0,1:T(2,128)S(1)}, bf16[8,128,256]{2,1,0:T(8,128)(2,1)S(1)}, s32[]{:T(128)}) %tuple.84), condition=%wide.while_cond, body=%wide.while_body.sunk | while | flops 2 | bytes 131177 | solution.py:56
  126.1 17.3 %while.32 = (s32[]{:T(128)}, bf16[2304,256]{1,0:T(8,128)(2,1)}, s32[8,2]{0,1:T(2,128)S(1)}, bf16[8,128,256]{2,1,0:T(8,128)(2,1)S(1)}, s32[]{:T(128)}) while((s32[]{:T(128)}, bf16[2304,256]{1,0:T(8,128)(2,1)}, s32[8,2]{0,1:T(2,128)S(1)}, bf16[8,128,256]{2,1,0:T(8,128)(2,1)S(1)}, s32[]{:T(128)}) %tuple.84), condition=%wide.while_cond, body=%wide.while_body.sunk | while | flops 2 | bytes 131177 | solution.py:56
  149.1 17.3 %while.32 = (s32[]{:T(128)}, bf16[2304,256]{1,0:T(8,128)(2,1)}, s32[8,2]{0,1:T(2,128)S(1)}, bf16[8,128,256]{2,1,0:T(8,128)(2,1)S(1)}, s32[]{:T(128)}) while((s32[]{:T(128)}, bf16[2304,256]{1,0:T(8,128)(2,1)}, s32[8,2]{0,1:T(2,128)S(1)}, bf16[8,128,256]{2,1,0:T(8,128)(2,1)S(1)}, s32[]{:T(128)}) %tuple.84), condition=%wide.while_cond, body=%wide.while_body.sunk | while | flops 2 | bytes 131177 | solution.py:56
  172.1 17.3 %while.32 = (s32[]{:T(128)}, bf16[2304,256]{1,0:T(8,128)(2,1)}, s32[8,2]{0,1:T(2,128)S(1)}, bf16[8,128,256]{2,1,0:T(8,128)(2,1)S(1)}, s32[]{:T(128)}) while((s32[]{:T(128)}, bf16[2304,256]{1,0:T(8,128)(2,1)}, s32[8,2]{0,1:T(2,128)S(1)}, bf16[8,128,256]{2,1,0:T(8,128)(2,1)S(1)}, s32[]{:T(128)}) %tuple.84), condition=%wide.while_cond, body=%wide.while_body.sunk | while | flops 2 | bytes 131177 | solution.py:56
  195.2 17.3 %while.32 = (s32[]{:T(128)}, bf16[2304,256]{1,0:T(8,128)(2,1)}, s32[8,2]{0,1:T(2,128)S(1)}, bf16[8,128,256]{2,1,0:T(8,128)(2,1)S(1)}, s32[]{:T(128)}) while((s32[]{:T(128)}, bf16[2304,256]{1,0:T(8,128)(2,1)}, s32[8,2]{0,1:T(2,128)S(1)}, bf16[8,128,256]{2,1,0:T(8,128)(2,1)S(1)}, s32[]{:T(128)}) %tuple.84), condition=%wide.while_cond, body=%wide.while_body.sunk | while | flops 2 | bytes 131177 | solution.py:56
  218.2 17.3 %while.32 = (s32[]{:T(128)}, bf16[2304,256]{1,0:T(8,128)(2,1)}, s32[8,2]{0,1:T(2,128)S(1)}, bf16[8,128,256]{2,1,0:T(8,128)(2,1)S(1)}, s32[]{:T(128)}) while((s32[]{:T(128)}, bf16[2304,256]{1,0:T(8,128)(2,1)}, s32[8,2]{0,1:T(2,128)S(1)}, bf16[8,128,256]{2,1,0:T(8,128)(2,1)S(1)}, s32[]{:T(128)}) %tuple.84), condition=%wide.while_cond, body=%wide.while_body.sunk | while | flops 2 | bytes 131177 | solution.py:56
  241.2 17.3 %while.32 = (s32[]{:T(128)}, bf16[2304,256]{1,0:T(8,128)(2,1)}, s32[8,2]{0,1:T(2,128)S(1)}, bf16[8,128,256]{2,1,0:T(8,128)(2,1)S(1)}, s32[]{:T(128)}) while((s32[]{:T(128)}, bf16[2304,256]{1,0:T(8,128)(2,1)}, s32[8,2]{0,1:T(2,128)S(1)}, bf16[8,128,256]{2,1,0:T(8,128)(2,1)S(1)}, s32[]{:T(128)}) %tuple.84), condition=%wide.while_cond, body=%wide.while_body.sunk | while | flops 2 | bytes 131177 | solution.py:56
  264.2 17.3 %while.32 = (s32[]{:T(128)}, bf16[2304,256]{1,0:T(8,128)(2,1)}, s32[8,2]{0,1:T(2,128)S(1)}, bf16[8,128,256]{2,1,0:T(8,128)(2,1)S(1)}, s32[]{:T(128)}) while((s32[]{:T(128)}, bf16[2304,256]{1,0:T(8,128)(2,1)}, s32[8,2]{0,1:T(2,128)S(1)}, bf16[8,128,256]{2,1,0:T(8,128)(2,1)S(1)}, s32[]{:T(128)}) %tuple.84), condition=%wide.while_cond, body=%wide.while_body.sunk | while | flops 2 | bytes 131177 | solution.py:56
  287.3 17.3 %while.32 = (s32[]{:T(128)}, bf16[2304,256]{1,0:T(8,128)(2,1)}, s32[8,2]{0,1:T(2,128)S(1)}, bf16[8,128,256]{2,1,0:T(8,128)(2,1)S(1)}, s32[]{:T(128)}) while((s32[]{:T(128)}, bf16[2304,256]{1,0:T(8,128)(2,1)}, s32[8,2]{0,1:T(2,128)S(1)}, bf16[8,128,256]{2,1,0:T(8,128)(2,1)S(1)}, s32[]{:T(128)}) %tuple.84), condition=%wide.while_cond, body=%wide.while_body.sunk | while | flops 2 | bytes 131177 | solution.py:56
  310.1 20.2 %reduce-scatter.3.cloned.1.call-done = bf16[256,256]{1,0:T(8,128)(2,1)} async-done(((bf16[1024,256]{1,0:T(8,128)(2,1)}), bf16[256,256]{1,0:T(8,128)(2,1)}) %reduce-scatter.3.cloned.1.call-update) | async-done | bytes 131088 | tf_op jit(solution)/shard_map/reduce_scatter | solution.py:114
  334.6 6.6 %all_gather.7 = bf16[1024,256]{1,0:T(8,128)(2,1)S(1)} all-gather(bf16[256,256]{1,0:T(8,128)(2,1)S(1)} %fusion.42), channel_id=1, replica_groups=mesh['row'=8,'col'=4] {'col'}, dimensions={0}, use_global_device_ids=true | all-gather | bytes 655360 | tf_op jit(solution)/shard_map/all_gather | solution.py:140
  341.2 26.8 %all-reduce.8.cloned.1.call-done = (f32[256,256]{0,1:T(8,128)}, f32[256,256]{0,1:T(8,128)}) async-done(((f32[256,256]{0,1:T(8,128)}, f32[256,256]{0,1:T(8,128)}), (f32[256,256]{0,1:T(8,128)}, f32[256,256]{0,1:T(8,128)})) %all-reduce.8.cloned.1.call-update) | async-done | bytes 524304 | tf_op jit(solution)/shard_map/psum | solution.py:134
  369.6 87.0 %while.31 = (s32[]{:T(128)}, f32[16,128,256]{2,1,0:T(8,128)}, s32[]{:T(128)}, s32[]{:T(128)}, s32[88]{0:T(128)S(1)}, /*index=5*/s32[88,16,128]{2,1,0:T(8,128)}, ...) while((s32[]{:T(128)}, f32[16,128,256]{2,1,0:T(8,128)}, s32[]{:T(128)}, ...), condition=%wide.region_8.9_spmd.clone, body=%wide.region_6.8_spmd.clone.sunk | while | flops 67897608 | bytes 5974609 | solution.py:101
  374.2 3.3 scatter_fusion
  397.7 3.3 scatter_fusion
  413.5 3.3 scatter_fusion
  421.5 3.3 scatter_fusion
  429.4 3.4 scatter_fusion
  453.1 3.5 scatter_fusion
  462.0 61.9 %reduce-scatter.5.cloned.1.call-done = bf16[256,256]{1,0:T(8,128)(2,1)} async-done(((bf16[2048,256]{1,0:T(8,128)(2,1)}), bf16[256,256]{1,0:T(8,128)(2,1)}) %reduce-scatter.5.cloned.1.call-update) | async-done | bytes 131088 | tf_op jit(solution)/shard_map/reduce_scatter | solution.py:142
  (588 shorter events, 320.7 us)
Async XLA Ops:
  7.2 323.2 %copy-start = (bf16[256,256]{1,0:T(8,128)(2,1)S(1)}, bf16[256,256]{1,0:T(8,128)(2,1)}, u32[]{:S(2)}) copy-start(bf16[256,256]{1,0:T(8,128)(2,1)} %param.17) | copy-start | bytes 393220
  7.2 48.4 %copy-start.1 = (s32[1,1,88]{2,1,0:T(1,128)S(1)}, s32[1,1,88]{2,1,0:T(1,128)}, u32[]{:S(2)}) copy-start(s32[1,1,88]{2,1,0:T(1,128)} %param.19) | copy-start | bytes 1060
  7.2 46.0 %all-gather.2.cloned.1.call-start = ((), (), s32[]{:S(2)}) async-start(), calls=%async_computation.2 | async-start | bytes 1179648 | tf_op jit(solution)/shard_map/all_gather | solution.py:112
  7.9 322.4 %reduce-scatter.3.cloned.1.call-start = ((), (), s32[]{:S(2)}) async-start(), calls=%async_computation.3 | async-start | bytes 655360 | tf_op jit(solution)/shard_map/reduce_scatter | solution.py:114
  308.9 1.0 copy-start.4
  308.9 1.0 copy-start.2
  308.9 1.0 copy-start.3
  308.9 21.4 %copy-start.5 = (bf16[256,256]{1,0:T(8,128)(2,1)S(1)}, bf16[256,256]{1,0:T(8,128)(2,1)}, u32[]{:S(2)}) copy-start(bf16[256,256]{1,0:T(8,128)(2,1)} %param.14) | copy-start | bytes 393220
  309.0 21.4 %copy-start.7 = (f32[256]{0:T(256)S(1)}, f32[256]{0:T(256)}, u32[]{:S(2)}) copy-start(f32[256]{0:T(256)} %param.18) | copy-start | bytes 3076
  309.8 58.1 %all-reduce.8.cloned.1.call-start = ((), (), s32[]{:S(2)}) async-start(), calls=%async_computation.6 | async-start | bytes 1048576 | tf_op jit(solution)/shard_map/psum | solution.py:134
  330.4 2.9 copy-start.6
  334.3 125.0 %all-reduce.6.cloned.1.call-start = ((), (), s32[]{:S(2)}) async-start(), calls=%async_computation.5 | async-start | bytes 1048576 | tf_op jit(solution)/shard_map/psum | solution.py:134
  368.0 156.0 %reduce-scatter.5.cloned.1.call-start = ((), (), s32[]{:S(2)}) async-start(), calls=%async_computation.4 | async-start | bytes 1179648 | tf_op jit(solution)/shard_map/reduce_scatter | solution.py:142
Sparse Core Ops, SparseCore 0:
  10.1 42.9 all-gather.1
  310.0 20.3 reduce-scatter.2
  334.4 33.4 all-reduce.7
  371.3 72.9 all-reduce.5
  459.4 64.5 reduce-scatter.4
